TPU v7x, 256 devices: a whole 4x4x8 slice. The times are simulated.
256 devices in a mesh: blk: 32 (over y_lo, z, core), grp: 8 (over y_hi, x).
Axes of the slice: x: 4, y: 4 (y_hi: 2, y_lo: 2; y = y_hi * 2 + y_lo), z: 8, core: 2. Of those that a mesh axis runs over, the one named last changes fastest.
Arguments:
- matrix_sat: float32 [2048, 131072], P('grp', 'blk'), may hold values from -0.046875 to 0.046875
- matrix_ter: float32 [2048, 131072], P('grp', 'blk'), may hold values from -0.046875 to 0.046875
- probes: float32 [16, 131072], P(None, 'blk'), may hold values from -6 to 6
Outputs:
- row_part: float32 [2, 16, 2048], P(None, None, 'grp')
- column_part: float32 [2, 16, 131072], P(None, None, ('blk', 'grp'))
- trace_terms: float32 [2, 16], replicated
All inputs are finite; a program needn't handle non-finite values.
Results may differ from a plain program's by a relative error of at most 0.000096.
Values sent between devices are 32-bit elements; how exact they have to be, the bound alone decides.
No kernel may reach another device: no remote copies, remote signals or barrier semaphores. Data moves between devices by JAX's collectives and lax.ppermute only.
A program may use at most 64 MiB of HBM per device.

v0:
```python
import jax
import jax.numpy as jnp
from jax import lax
from jax.sharding import Mesh
from jax.sharding import PartitionSpec as P

BLK = ("blk_0", "blk_1", "blk_2")
GRP = ("grp_0", "grp_1")
BLK_GRP = ("blk_0", "blk_1", "blk_2", "grp_0", "grp_1")


def from_root(shard, axis, root):
    return lax.dynamic_index_in_dim(lax.all_gather(shard, axis), root, 0, keepdims=False)


def one_axis_at_a_time(shard, axes):
    for axis in axes:
        shard = lax.psum(shard, axis)
    return shard


def total_of_pieces(shard, axis):
    return lax.all_gather(shard, axis).sum(0)


def cut_along(shard, dim, size):
    dims = shard.shape
    blocks = shard.reshape(*dims[:dim], size, dims[dim] // size, *dims[dim + 1 :])
    return jnp.moveaxis(blocks, dim, 0)


def summed_on_arrival(shard, axis, dim):
    blocks = cut_along(shard, dim, lax.axis_size(axis))
    arrived = lax.all_to_all(blocks, axis, split_axis=0, concat_axis=0, tiled=True)
    return arrived.sum(axis=0)


def shards(matrix_sat, matrix_ter, probes):
    rows_dev, cols_dev = matrix_sat.shape
    column_index = lax.axis_index(BLK)
    row_index = lax.axis_index(GRP)
    row_ids = row_index * rows_dev + lax.broadcasted_iota(jnp.int32, (rows_dev, cols_dev), 0)
    col_ids = column_index * cols_dev + lax.broadcasted_iota(jnp.int32, (rows_dev, cols_dev), 1)
    upper_mask = col_ids >= row_ids
    strict_mask = col_ids > row_ids
    mine = lax.dynamic_slice_in_dim(probes, row_index * rows_dev, rows_dev, 1)
    slab_probes = from_root(mine, BLK, 0)
    hp = lax.Precision.HIGHEST
    direct_list = []
    mirror_list = []
    for matrix in (matrix_sat, matrix_ter):
        masked_upper = jnp.where(upper_mask, matrix, 0.0)
        masked_strict = jnp.where(strict_mask, matrix, 0.0)
        direct_list.append(
            lax.dot_general(probes, masked_upper, (((1,), (1,)), ((), ())), precision=hp)
        )
        mirror_list.append(jnp.dot(slab_probes, masked_strict, precision=hp))
    direct_terms = jnp.stack(direct_list)
    mirror_terms = jnp.stack(mirror_list)
    early_local = jnp.sum(slab_probes[None] * direct_terms, axis=2) + jnp.sum(
        probes[None] * mirror_terms, axis=2
    )
    early_trace = one_axis_at_a_time(early_local, BLK_GRP)
    row_part = total_of_pieces(direct_terms, BLK)
    column_part = summed_on_arrival(mirror_terms, GRP, 2)
    return (row_part, column_part, early_trace)


def solution(mesh):
    split = Mesh(mesh.devices.reshape(2, 8, 2, 2, 4), ("blk_0", "blk_1", "blk_2", "grp_0", "grp_1"))
    in_specs = (P(GRP, BLK), P(GRP, BLK), P(None, BLK))
    out_specs = (P(None, None, GRP), P(None, None, BLK_GRP), P())
    return jax.shard_map(
        shards, mesh=split, in_specs=in_specs, out_specs=out_specs, check_vma=False
    )
```

profile of v0, /device:TPU:2, one launch (start us, length us, event | category | flops | bytes accessed | tf_op | source)
XLA Modules:
  0.0 125.4 jit_solution(13252278011082796991)
XLA Ops:
  7.2 0.0 all-gather.4.cloned.1.call-start
  7.3 0.9 constant_dynamic-slice_fusion
  8.2 5.8 %fusion.16 = f32[1,16,256]{2,1,0:T(8,128)S(1)} fusion(f32[16,4096]{1,0:T(8,128)} %param.5, f32[256,4096]{1,0:T(8,128)} %param.4, s32[4096]{0:T(1024)S(1)} %iota_add_fusion, s32[256]{0:T(256)S(1)} %iota_add_fusion.1), kind=kOutput, calls=%fused_computation.20 | convolution fusion | flops 203423744 | bytes 4490240 | tf_op jit(solution)/shard_map/dot_general | solution.py:55
  14.0 3.5 %fusion.17 = f32[1,16,256]{2,1,0:T(8,128)S(1)} fusion(f32[16,4096]{1,0:T(8,128)S(1)} %copy-done.2, f32[256,4096]{1,0:T(8,128)S(1)} %copy-done, s32[4096]{0:T(1024)S(1)} %iota_add_fusion, s32[256]{0:T(256)S(1)} %iota_add_fusion.1), kind=kOutput, calls=%fused_computation.21 | convolution fusion | flops 203423744 | bytes 4490240 | tf_op jit(solution)/shard_map/dot_general | solution.py:55
  17.5 38.6 %all-gather.1 = f32[512,256]{1,0:T(8,128)S(1)} all-gather(f32[16,256]{1,0:T(8,128)S(1)} %constant_dynamic-slice_fusion), channel_id=3, replica_groups=mesh['blk_0'=2,'blk_1'=8,'blk_2'=2,'grp_0'=2,'grp_1'=4] {'blk_0','blk_1'..., dimensions={0}, use_global_device_ids=true | all-gather | bytes 540672 | tf_op jit(solution)/shard_map/all_gather | solution.py:13
  56.1 0.6 multiply_reduce_fusion
  56.7 0.0 all-gather.4.cloned.1.call-update
  56.8 4.7 %fusion.2 = f32[16,4096]{1,0:T(8,128)S(1)} fusion(f32[256,4096]{1,0:T(8,128)} %param.3, s32[4096]{0:T(1024)S(1)} %iota_add_fusion, s32[256]{0:T(256)S(1)} %iota_add_fusion.1, f32[512,256]{1,0:T(8,128)S(1)} %all-gather.1), kind=kOutput, calls=%fused_computation.6 | convolution fusion | flops 203423744 | bytes 4490240 | tf_op jit(solution)/shard_map/dot_general | solution.py:57
  61.5 0.2 copy.8
  61.6 0.2 copy.6
  61.8 2.4 %fusion.3 = f32[16,4096]{1,0:T(8,128)S(1)} fusion(f32[256,4096]{1,0:T(8,128)S(1)} %copy-done.1, s32[4096]{0:T(1024)S(1)} %iota_add_fusion, s32[256]{0:T(256)S(1)} %iota_add_fusion.1, f32[512,256]{1,0:T(8,128)S(1)} %all-gather.1), kind=kOutput, calls=%fused_computation.7 | convolution fusion | flops 203423744 | bytes 4490240 | tf_op jit(solution)/shard_map/dot_general | solution.py:57
  64.2 0.2 copy.9
  64.4 0.2 copy.7
  64.5 0.9 maximum_bitcast_fusion
  65.4 7.2 %all-to-all-start = ((f32[8,2,16,512]{3,2,1,0:T(8,128)}), f32[8,2,16,512]{3,2,1,0:T(8,128)S(1)}, u32[]{:S(2)}, u32[]{:S(2)}) async-start(f32[8,2,16,512]{3,2,1,0:T(8,128)} %maximum_bitcast_fusion), calls=%async_computation | async-start | bytes 1048576 | tf_op jit(solution)/shard_map/all_to_all | solution.py:34
  72.5 0.1 fusion.18
  72.7 5.5 %psum.35 = f32[2,16]{1,0:T(2,128)S(1)} all-reduce(f32[2,16]{1,0:T(2,128)S(1)} %add.49), channel_id=1, replica_groups=mesh['blk_0'=2,'blk_1'=8,'blk_2'=2,'grp_0'=2,'grp_1'=4] {'blk_0'}, use_global_device_ids=true, to_apply=%region_4.5 | all-reduce | flops 32 | bytes 256 | tf_op jit(solution)/shard_map/psum | solution.py:18
  78.2 14.2 %psum.36 = f32[2,16]{1,0:T(2,128)S(1)} all-reduce(f32[2,16]{1,0:T(2,128)S(1)} %psum.35), channel_id=1, replica_groups=mesh['blk_0'=2,'blk_1'=8,'blk_2'=2,'grp_0'=2,'grp_1'=4] {'blk_1'}, use_global_device_ids=true, to_apply=%region_5.6 | all-reduce | flops 32 | bytes 256 | tf_op jit(solution)/shard_map/psum | solution.py:18
  92.4 2.5 %psum.37 = f32[2,16]{1,0:T(2,128)S(1)} all-reduce(f32[2,16]{1,0:T(2,128)S(1)} %psum.36), channel_id=1, replica_groups=mesh['blk_0'=2,'blk_1'=8,'blk_2'=2,'grp_0'=2,'grp_1'=4] {'blk_2'}, use_global_device_ids=true, to_apply=%region_6.7 | all-reduce | flops 32 | bytes 256 | tf_op jit(solution)/shard_map/psum | solution.py:18
  94.9 6.4 %psum.38 = f32[2,16]{1,0:T(2,128)S(1)} all-reduce(f32[2,16]{1,0:T(2,128)S(1)} %psum.37), channel_id=1, replica_groups=mesh['blk_0'=2,'blk_1'=8,'blk_2'=2,'grp_0'=2,'grp_1'=4] {'grp_0'}, use_global_device_ids=true, to_apply=%region_7.8 | all-reduce | flops 32 | bytes 256 | tf_op jit(solution)/shard_map/psum | solution.py:18
  101.3 10.6 %psum.39 = f32[2,16]{1,0:T(2,128)} all-reduce(f32[2,16]{1,0:T(2,128)S(1)} %psum.38), channel_id=1, replica_groups=mesh['blk_0'=2,'blk_1'=8,'blk_2'=2,'grp_0'=2,'grp_1'=4] {'grp_1'}, use_global_device_ids=true, to_apply=%region_8.9 | all-reduce | flops 32 | bytes 256 | tf_op jit(solution)/shard_map/psum | solution.py:18
  111.9 0.7 reduce_sum.37
  112.6 4.0 %all-gather.4.cloned.1.call-done = f32[64,16,256]{2,1,0:T(8,128)} async-done(((f32[2,16,256]{2,1,0:T(8,128)}), f32[64,16,256]{2,1,0:T(8,128)}) %all-gather.4.cloned.1.call-update) | async-done | bytes 1048592 | tf_op jit(solution)/shard_map/all_gather | solution.py:23
  116.6 1.9 %reduce_sum.36 = f32[2,16,256]{2,1,0:T(8,128)} reduce(f32[32,2,16,256]{3,2,1,0:T(8,128)} %bitcast.25, f32[]{:T(128)} %constant.37.clone.1), dimensions={0}, to_apply=%region_0.1 | reduce | flops 253952 | bytes 1081348 | tf_op jit(solution)/shard_map/reduce_sum | solution.py:23
  (11 shorter events, 0.1 us)
Async XLA Ops:
  7.2 6.8 %copy-start.2 = (f32[16,4096]{1,0:T(8,128)S(1)}, f32[16,4096]{1,0:T(8,128)}, u32[]{:S(2)}) copy-start(f32[16,4096]{1,0:T(8,128)} %param.5) | copy-start | bytes 786436
  7.2 109.4 %all-gather.4.cloned.1.call-start = ((), (), s32[]{:S(2)}) async-start(), calls=%async_computation.1 | async-start | bytes 1081344 | tf_op jit(solution)/shard_map/all_gather | solution.py:23
  7.3 6.8 %copy-start = (f32[256,4096]{1,0:T(8,128)S(1)}, f32[256,4096]{1,0:T(8,128)}, u32[]{:S(2)}) copy-start(f32[256,4096]{1,0:T(8,128)} %param.3) | copy-start | bytes 12582916
  56.8 5.0 %copy-start.1 = (f32[256,4096]{1,0:T(8,128)S(1)}, f32[256,4096]{1,0:T(8,128)}, u32[]{:S(2)}) copy-start(f32[256,4096]{1,0:T(8,128)} %param.4) | copy-start | bytes 12582916
  65.4 46.5 %all-to-all-start = ((f32[8,2,16,512]{3,2,1,0:T(8,128)}), f32[8,2,16,512]{3,2,1,0:T(8,128)S(1)}, u32[]{:S(2)}, u32[]{:S(2)}) async-start(f32[8,2,16,512]{3,2,1,0:T(8,128)} %maximum_bitcast_fusion), calls=%async_computation | async-start | bytes 1048576 | tf_op jit(solution)/shard_map/all_to_all | solution.py:34
Sparse Core Ops, SparseCore 0:
  56.9 59.6 all-gather.3
where the time goes:
time: 127 us; the launch traced here: 125 us
  blocking collectives  77.8 us (61%)
  matrix products  16.4 us (13%)
  between operations  14.1 us (11%)
  starting transfers between devices  7.2 us (6%)
  other arithmetic  4.22 us (3%)
  waiting for transfers between devices  4.04 us (3%)
  local copies, waits for them, and re-layouts  1.54 us (1%)
    psum x5, blocking collectives, one_axis_at_a_time(): shard = lax.psum(shard, axis)  39.2 us
    all_gather x1, blocking collectives, from_root(): lax.all_gather(shard, axis)  38.6 us
    dot_general x2, matrix products, shards(): lax.dot_general(probes, masked_upper, (((1,), (1,)), ((), ())), precision...  9.3 us
    all_to_all x1, starting transfers between devices, summed_on_arrival(): lax.all_to_all(blocks, axis, split_axis=0, concat_axis=0, tiled=True)  7.17 us
    dot_general x2, matrix products, shards(): mirror_list.append(jnp.dot(slab_probes, masked_strict, precision=hp))  7.08 us
    all_gather x1, waiting for transfers between devices, total_of_pieces(): return lax.all_gather(shard, axis).sum(0)  4.02 us
  transfers between devices with their start and end apart: 2, of which 1 were waited for; matrix products, arithmetic and copies ran while one was open for 7% of the time, Pallas kernels for 0%

commit v1 on v0

v1 whole, which is shorter than its diff:
```python
import functools

import jax
import jax.numpy as jnp
from jax import lax
from jax.experimental import pallas as pl
from jax.experimental.pallas import tpu as pltpu
from jax.sharding import Mesh
from jax.sharding import PartitionSpec as P

BLK = ("blk_0", "blk_1", "blk_2")
GRP = ("grp_0", "grp_1")
BLK_GRP = BLK + GRP
WIDTH = 1024
f32, bf16 = jnp.float32, jnp.bfloat16
VMEM = pl.BlockSpec(memory_space=pltpu.VMEM)


def halves(value):
    high = value.astype(bf16)
    return high, (value - high.astype(f32)).astype(bf16)


def stacked_halves(value):
    return jnp.concatenate(halves(value), axis=0)


def fold(both):
    half = both.shape[0] // 2
    return both[:half] + both[half:]


def dot_rows(probes_hl, matrix):
    high, low = halves(matrix)
    dims = (((1,), (1,)), ((), ()))
    return fold(
        lax.dot_general(probes_hl, high, dims, preferred_element_type=f32)
        + lax.dot_general(probes_hl, low, dims, preferred_element_type=f32)
    )


def dot_columns(slab_hl, matrix):
    high, low = halves(matrix)
    return fold(
        jnp.dot(slab_hl, high, preferred_element_type=f32)
        + jnp.dot(slab_hl, low, preferred_element_type=f32)
    )


def offsets(rows, cols):
    return lax.axis_index(GRP) * rows, lax.axis_index(BLK) * cols


def ids(shape, row0, col0):
    return (
        row0 + lax.broadcasted_iota(jnp.int32, shape, 0),
        col0 + lax.broadcasted_iota(jnp.int32, shape, 1),
    )


def row_kernel(cols, sat, ter, probes, out):
    step = pl.program_id(0)
    rows = sat.shape[0]
    n = probes.shape[0]
    row0, dev_col0 = offsets(rows, cols)
    col0 = dev_col0 + step * WIDTH

    @pl.when(step == 0)
    def _():
        out[...] = jnp.zeros_like(out)

    probes_hl = stacked_halves(probes[...])
    crossed = col0 < row0 + rows

    @pl.when(jnp.logical_not(crossed))
    def _():
        for k, matrix in enumerate((sat, ter)):
            out[k * n : (k + 1) * n] += dot_rows(probes_hl, matrix[...])

    @pl.when(crossed)
    def _():
        r, c = ids(sat.shape, row0, col0)
        for k, matrix in enumerate((sat, ter)):
            kept = jnp.where(c >= r, matrix[...], 0.0)
            out[k * n : (k + 1) * n] += dot_rows(probes_hl, kept)

    @pl.when((row0 >= col0) & (row0 < col0 + WIDTH))
    def _():
        at = pl.ds(pl.multiple_of(row0 - col0, rows), rows)
        out[2 * n : 3 * n] = probes[:, at]
        r, c = ids((rows, rows), 0, 0)
        for k, matrix in enumerate((sat, ter)):
            diagonal = jnp.sum(jnp.where(r == c, matrix[:, at], 0.0), axis=0, keepdims=True)
            out[3 * n + k : 3 * n + k + 1] = diagonal


def row_products(sat, ter, probes):
    rows, cols = sat.shape
    n = probes.shape[0]
    return pl.pallas_call(
        functools.partial(row_kernel, cols),
        grid=(cols // WIDTH,),
        in_specs=[
            pl.BlockSpec((rows, WIDTH), lambda j: (0, j)),
            pl.BlockSpec((rows, WIDTH), lambda j: (0, j)),
            pl.BlockSpec((n, WIDTH), lambda j: (0, j)),
        ],
        out_specs=pl.BlockSpec((3 * n + 8, rows), lambda j: (0, 0)),
        out_shape=jax.ShapeDtypeStruct((3 * n + 8, rows), f32),
        name="row_products",
    )(sat, ter, probes)


def column_kernel(cols, n, parts, sat, ter, shared, out, row_part):
    step = pl.program_id(0)
    rows = sat.shape[0]
    row0, dev_col0 = offsets(rows, cols)
    col0 = dev_col0 + step * WIDTH
    slab = shared[2 * n : 3 * n]
    slab_hl = stacked_halves(slab)
    groups = cols // parts // 128
    first = step * (WIDTH // (cols // parts))

    def place(k, result):
        for q in range(WIDTH // 128):
            at = (q % groups) * 2 * n + k * n
            out[first + q // groups, at : at + n] = result[:, q * 128 : (q + 1) * 128]

    crossed = col0 <= row0 + rows - 1

    @pl.when(jnp.logical_not(crossed))
    def _():
        for k, matrix in enumerate((sat, ter)):
            place(k, dot_columns(slab_hl, matrix[...]))

    @pl.when(crossed)
    def _():
        r, c = ids(sat.shape, row0, col0)
        for k, matrix in enumerate((sat, ter)):
            place(k, dot_columns(slab_hl, jnp.where(c > r, matrix[...], 0.0)))

    @pl.when(step == 0)
    def _():
        eye = jnp.equal(*ids((n, 128), 0, 0))
        tail = []
        for k in range(2):
            direct = shared[k * n : (k + 1) * n]
            row_part[k] = direct
            diagonal = shared[3 * n + k : 3 * n + k + 1]
            term = jnp.sum(slab * (2.0 * direct - diagonal * slab), axis=1, keepdims=True)
            tail.append(jnp.sum(jnp.where(eye, term, 0.0), axis=0, keepdims=True))
        tail.append(jnp.zeros((6, 128), f32))
        tail = jnp.concatenate(tail, axis=0)
        for part in range(parts):
            out[part, groups * 2 * n : groups * 2 * n + 8] = tail


def column_products(sat, ter, shared, n, parts):
    rows, cols = sat.shape
    chunk = (cols // parts // 128) * 2 * n + 8
    return pl.pallas_call(
        functools.partial(column_kernel, cols, n, parts),
        grid=(cols // WIDTH,),
        in_specs=[
            pl.BlockSpec((rows, WIDTH), lambda j: (0, j)),
            pl.BlockSpec((rows, WIDTH), lambda j: (0, j)),
            pl.BlockSpec(shared.shape, lambda j: (0, 0)),
        ],
        out_specs=[
            pl.BlockSpec((parts, chunk, 128), lambda j: (0, 0, 0)),
            pl.BlockSpec((2, n, rows), lambda j: (0, 0, 0)),
        ],
        out_shape=[
            jax.ShapeDtypeStruct((parts, chunk, 128), f32),
            jax.ShapeDtypeStruct((2, n, rows), f32),
        ],
        name="column_products",
    )(sat, ter, shared)


def sum_kernel(n, arrived, column_part, trace):
    parts, chunk, _ = arrived.shape
    groups = (chunk - 8) // (2 * n)
    total = arrived[0]
    for part in range(1, parts):
        total = total + arrived[part]
    for q in range(groups):
        for k in range(2):
            at = q * 2 * n + k * n
            column_part[k, :, q * 128 : (q + 1) * 128] = total[at : at + n]
    trace[...] = total[groups * 2 * n : groups * 2 * n + 2, :n]


def sum_parts(arrived, n, width):
    return pl.pallas_call(
        functools.partial(sum_kernel, n),
        in_specs=[VMEM],
        out_specs=[VMEM, VMEM],
        out_shape=[
            jax.ShapeDtypeStruct((2, n, width), f32),
            jax.ShapeDtypeStruct((2, n), f32),
        ],
        name="sum_parts",
    )(arrived)


def exchanged_sum(value, axis, bit):
    size = lax.axis_size(axis)
    return value + lax.ppermute(value, axis, [(i, i ^ bit) for i in range(size)])


def shards(matrix_sat, matrix_ter, probes):
    n, cols = probes.shape
    shared = row_products(matrix_sat, matrix_ter, probes)
    for axis in ("blk_2", "blk_0", "blk_1"):
        bit = 1
        while bit < lax.axis_size(axis):
            shared = exchanged_sum(shared, axis, bit)
            bit *= 2
    parts = lax.axis_size(GRP)
    mirrored, row_part = column_products(matrix_sat, matrix_ter, shared, n, parts)
    arrived = lax.all_to_all(mirrored, GRP, split_axis=0, concat_axis=0, tiled=True)
    column_part, trace_terms = sum_parts(arrived, n, cols // parts)
    return row_part, column_part, trace_terms


def solution(mesh):
    split = Mesh(mesh.devices.reshape(2, 8, 2, 2, 4), BLK_GRP)
    in_specs = (P(GRP, BLK), P(GRP, BLK), P(None, BLK))
    out_specs = (P(None, None, GRP), P(None, None, BLK_GRP), P())
    return jax.shard_map(
        shards, mesh=split, in_specs=in_specs, out_specs=out_specs, check_vma=False
    )
```

time: 127 us -> 58.5 us (0.46); the launches traced: 125 us -> 58.2 us
  blocking collectives: 77.8 us -> 16.9 us
  matrix products: 16.4 us -> 0 us
  Pallas kernels: 0 us -> 13.9 us
  between operations: 14.1 us -> 0.65 us
  waiting for transfers between devices: 4.04 us -> 11.2 us
  starting transfers between devices: 7.2 us -> 14.1 us
  other arithmetic: 4.22 us -> 1.48 us
  local copies, waits for them, and re-layouts: 1.54 us -> 0 us
    psum x5 -> x0, blocking collectives: 39.2 us -> none  [one_axis_at_a_time(): shard = lax.psum(shard, axis)]
    all_gather x1 -> x0, blocking collectives: 38.6 us -> none  [from_root(): lax.all_gather(shard, axis)]
    all_to_all x0 -> x1, blocking collectives: none -> 16.9 us  [shards(): lax.all_to_all(mirrored, GRP, split_axis=0, concat_axis=0, tiled=True)]
    dot_general x4 -> x0, matrix products: 16.4 us -> none  [the longest x2 9.3 us: shards(): lax.dot_general(probes, masked_upper, (((1,), (1,)), ((), ())), precision...]
    ppermute x0 -> x5, starting transfers between devices: none -> 14.1 us  [exchanged_sum(): lax.ppermute(value, axis, [(i, i ^ bit) for i in range(size)])]
    pallas_call x0 -> x3, Pallas kernels: none -> 13.9 us  [the longest x1 6.21 us: row_products(): pl.pallas_call(functools.partial(row_kernel, cols), grid=(cols // WIDTH,)...]
    ppermute x0 -> x5, waiting for transfers between devices: none -> 11.2 us  [exchanged_sum(): lax.ppermute(value, axis, [(i, i ^ bit) for i in range(size)])]
    all_to_all x1 -> x0, starting transfers between devices: 7.17 us -> none  [summed_on_arrival(): lax.all_to_all(blocks, axis, split_axis=0, concat_axis=0, tiled=True)]
  transfers between devices with their start and end apart: 2 -> 5, of which waited for: 1 -> 5; matrix products, arithmetic and copies ran while one was open for 7% -> 0% of each run, Pallas kernels for 0% -> 0%
where the time goes in v1:
time: 58.5 us; the launch traced here: 58.2 us
  blocking collectives  16.9 us (29%)
  starting transfers between devices  14.1 us (24%)
  Pallas kernels  13.9 us (24%)
  waiting for transfers between devices  11.2 us (19%)
  other arithmetic  1.48 us (3%)
  between operations  0.65 us (1%)
    all_to_all x1, blocking collectives, shards(): lax.all_to_all(mirrored, GRP, split_axis=0, concat_axis=0, tiled=True)  16.9 us
    ppermute x5, starting transfers between devices, exchanged_sum(): lax.ppermute(value, axis, [(i, i ^ bit) for i in range(size)])  14.1 us
    ppermute x5, waiting for transfers between devices, exchanged_sum(): lax.ppermute(value, axis, [(i, i ^ bit) for i in range(size)])  11.2 us
    pallas_call x1, Pallas kernels, row_products(): pl.pallas_call(functools.partial(row_kernel, cols), grid=(cols // WIDTH,)...  6.21 us
    pallas_call x1, Pallas kernels, column_products(): pl.pallas_call(functools.partial(column_kernel, cols, n, parts), grid=(co...  5.99 us
    pallas_call x1, Pallas kernels, sum_parts(): pl.pallas_call(functools.partial(sum_kernel, n), in_specs=[VMEM], out_spe...  1.71 us
    add x5, other arithmetic, exchanged_sum(): value + lax.ppermute(value, axis, [(i, i ^ bit) for i in range(size)])  1.48 us
  transfers between devices with their start and end apart: 5, of which 5 were waited for; matrix products, arithmetic and copies ran while one was open for 0% of the time, Pallas kernels for 0%

profile of v1, /device:TPU:2, one launch (start us, length us, event | category | flops | bytes accessed | tf_op | source)
XLA Modules:
  0.0 58.2 jit_solution(11615640579897437024)
XLA Ops:
  0.6 6.2 %row_products.1 = f32[56,256]{1,0:T(8,128)} custom-call(f32[256,4096]{1,0:T(8,128)} %sat.3, f32[256,4096]{1,0:T(8,128)} %ter.3, f32[16,4096]{1,0:T(8,128)} %probes.1), custom_call_target="tpu_custom_call" | custom-call | tf_op jit(solution)/shard_map/row_products/pallas_call | solution.py:100
  6.8 0.0 collective-permute-start
  6.8 1.4 %collective-permute-done = f32[56,256]{1,0:T(8,128)S(1)} collective-permute-done((f32[56,256]{1,0:T(8,128)}, f32[56,256]{1,0:T(8,128)S(1)}, u32[]{:S(2)}, u32[]{:S(2)}) %collective-permute-start) | collective-permute-done | bytes 57376 | tf_op jit(solution)/shard_map/ppermute | solution.py:209
  8.3 0.8 %add.15 = f32[56,256]{1,0:T(8,128)S(1)} add(f32[56,256]{1,0:T(8,128)} %row_products.1, f32[56,256]{1,0:T(8,128)S(1)} %collective-permute-done) | non-fusion elementwise | flops 14336 | bytes 172032 | tf_op jit(solution)/shard_map/add | solution.py:209
  9.1 1.4 %collective-permute-start.1 = (f32[56,256]{1,0:T(8,128)S(1)}, f32[56,256]{1,0:T(8,128)S(1)}, u32[]{:S(2)}, u32[]{:S(2)}) collective-permute-start(f32[56,256]{1,0:T(8,128)S(1)} %add.15), channel_id=1, source_target_pairs={{0,128},{128,0},{1,129},{129,1},{2,130},{130,2},{3,131},{131,3},{4... | collective-permute-start | bytes 172040 | tf_op jit(solution)/shard_map/ppermute | solution.py:209
  10.6 2.7 %collective-permute-done.1 = f32[56,256]{1,0:T(8,128)S(1)} collective-permute-done((f32[56,256]{1,0:T(8,128)S(1)}, f32[56,256]{1,0:T(8,128)S(1)}, u32[]{:S(2)}, u32[]{:S(2)}) %collective-permute-start.1) | collective-permute-done | bytes 57376 | tf_op jit(solution)/shard_map/ppermute | solution.py:209
  13.3 1.9 %collective-permute-start.2 = (f32[56,256]{1,0:T(8,128)S(1)}, f32[56,256]{1,0:T(8,128)S(1)}, u32[]{:S(2)}, u32[]{:S(2)}) collective-permute-start(f32[56,256]{1,0:T(8,128)S(1)} %add.16), channel_id=1, source_target_pairs={{0,16},{16,0},{32,48},{48,32},{64,80},{80,64},{96,112},{112,96},{1... | collective-permute-start | bytes 172040 | tf_op jit(solution)/shard_map/ppermute | solution.py:209
  15.2 2.4 %collective-permute-done.2 = f32[56,256]{1,0:T(8,128)S(1)} collective-permute-done((f32[56,256]{1,0:T(8,128)S(1)}, f32[56,256]{1,0:T(8,128)S(1)}, u32[]{:S(2)}, u32[]{:S(2)}) %collective-permute-start.2) | collective-permute-done | bytes 57376 | tf_op jit(solution)/shard_map/ppermute | solution.py:209
  17.6 3.2 %collective-permute-start.3 = (f32[56,256]{1,0:T(8,128)S(1)}, f32[56,256]{1,0:T(8,128)S(1)}, u32[]{:S(2)}, u32[]{:S(2)}) collective-permute-start(f32[56,256]{1,0:T(8,128)S(1)} %add.17), channel_id=1, source_target_pairs={{0,32},{16,48},{32,0},{48,16},{64,96},{80,112},{96,64},{112,80},{1... | collective-permute-start | bytes 172040 | tf_op jit(solution)/shard_map/ppermute | solution.py:209
  20.8 2.2 %collective-permute-done.3 = f32[56,256]{1,0:T(8,128)S(1)} collective-permute-done((f32[56,256]{1,0:T(8,128)S(1)}, f32[56,256]{1,0:T(8,128)S(1)}, u32[]{:S(2)}, u32[]{:S(2)}) %collective-permute-start.3) | collective-permute-done | bytes 57376 | tf_op jit(solution)/shard_map/ppermute | solution.py:209
  23.0 7.5 %collective-permute-start.4 = (f32[56,256]{1,0:T(8,128)S(1)}, f32[56,256]{1,0:T(8,128)S(1)}, u32[]{:S(2)}, u32[]{:S(2)}) collective-permute-start(f32[56,256]{1,0:T(8,128)S(1)} %add.18), channel_id=1, source_target_pairs={{0,64},{16,80},{32,96},{48,112},{64,0},{80,16},{96,32},{112,48},{1... | collective-permute-start | bytes 172040 | tf_op jit(solution)/shard_map/ppermute | solution.py:209
  30.5 2.5 %collective-permute-done.4 = f32[56,256]{1,0:T(8,128)S(1)} collective-permute-done((f32[56,256]{1,0:T(8,128)S(1)}, f32[56,256]{1,0:T(8,128)S(1)}, u32[]{:S(2)}, u32[]{:S(2)}) %collective-permute-start.4) | collective-permute-done | bytes 57376 | tf_op jit(solution)/shard_map/ppermute | solution.py:209
  33.0 0.6 %add.19.shared = f32[56,256]{1,0:T(8,128)} add(f32[56,256]{1,0:T(8,128)S(1)} %add.18, f32[56,256]{1,0:T(8,128)S(1)} %collective-permute-done.4) | non-fusion elementwise | flops 14336 | bytes 172032 | tf_op jit(solution)/shard_map/add | solution.py:209
  33.6 6.0 %column_products.1 = (f32[8,136,128]{2,1,0:T(8,128)}, f32[2,16,256]{2,1,0:T(8,128)}) custom-call(f32[256,4096]{1,0:T(8,128)} %sat.3, f32[256,4096]{1,0:T(8,128)} %ter.3, f32[56,256]{1,0:T(8,128)} %add.19.shared), custom_call_target="tpu_custom_call" | custom-call | tf_op jit(solution)/shard_map/column_products/pallas_call | solution.py:161
  39.6 16.9 %all_to_all.5.arrived = f32[8,136,128]{2,1,0:T(8,128)} all-to-all(f32[8,136,128]{2,1,0:T(8,128)} %get-tuple-element.8), channel_id=1, replica_groups=mesh['blk_0'=2,'blk_1'=8,'blk_2'=2,'grp_0'=2,'grp_1'=4] {'grp_0','grp_1'}, dimensions={0} | all-to-all | bytes 1114112 | tf_op jit(solution)/shard_map/all_to_all | solution.py:222
  56.5 1.7 %sum_parts.1 = (f32[2,16,512]{2,1,0:T(8,128)}, f32[2,16]{1,0:T(2,128)}) custom-call(f32[8,136,128]{2,1,0:T(8,128)} %all_to_all.5.arrived), custom_call_target="tpu_custom_call" | custom-call | tf_op jit(solution)/shard_map/sum_parts/pallas_call | solution.py:195
  (3 shorter events, 0.0 us)
Async XLA Ops:
  6.8 1.5 %collective-permute-start = (f32[56,256]{1,0:T(8,128)}, f32[56,256]{1,0:T(8,128)S(1)}, u32[]{:S(2)}, u32[]{:S(2)}) collective-permute-start(f32[56,256]{1,0:T(8,128)} %row_products.1), channel_id=1, source_target_pairs={{0,8},{8,0},{1,9},{9,1},{2,10},{10,2},{3,11},{11,3},{4,12},{12,4},... | collective-permute-start | bytes 172040 | tf_op jit(solution)/shard_map/ppermute | solution.py:209
  9.1 4.2 %collective-permute-start.1 = (f32[56,256]{1,0:T(8,128)S(1)}, f32[56,256]{1,0:T(8,128)S(1)}, u32[]{:S(2)}, u32[]{:S(2)}) collective-permute-start(f32[56,256]{1,0:T(8,128)S(1)} %add.15), channel_id=1, source_target_pairs={{0,128},{128,0},{1,129},{129,1},{2,130},{130,2},{3,131},{131,3},{4... | collective-permute-start | bytes 172040 | tf_op jit(solution)/shard_map/ppermute | solution.py:209
  13.3 4.3 %collective-permute-start.2 = (f32[56,256]{1,0:T(8,128)S(1)}, f32[56,256]{1,0:T(8,128)S(1)}, u32[]{:S(2)}, u32[]{:S(2)}) collective-permute-start(f32[56,256]{1,0:T(8,128)S(1)} %add.16), channel_id=1, source_target_pairs={{0,16},{16,0},{32,48},{48,32},{64,80},{80,64},{96,112},{112,96},{1... | collective-permute-start | bytes 172040 | tf_op jit(solution)/shard_map/ppermute | solution.py:209
  17.6 5.4 %collective-permute-start.3 = (f32[56,256]{1,0:T(8,128)S(1)}, f32[56,256]{1,0:T(8,128)S(1)}, u32[]{:S(2)}, u32[]{:S(2)}) collective-permute-start(f32[56,256]{1,0:T(8,128)S(1)} %add.17), channel_id=1, source_target_pairs={{0,32},{16,48},{32,0},{48,16},{64,96},{80,112},{96,64},{112,80},{1... | collective-permute-start | bytes 172040 | tf_op jit(solution)/shard_map/ppermute | solution.py:209
  23.0 10.0 %collective-permute-start.4 = (f32[56,256]{1,0:T(8,128)S(1)}, f32[56,256]{1,0:T(8,128)S(1)}, u32[]{:S(2)}, u32[]{:S(2)}) collective-permute-start(f32[56,256]{1,0:T(8,128)S(1)} %add.18), channel_id=1, source_target_pairs={{0,64},{16,80},{32,96},{48,112},{64,0},{80,16},{96,32},{112,48},{1... | collective-permute-start | bytes 172040 | tf_op jit(solution)/shard_map/ppermute | solution.py:209

commit v2 on v1

v2 whole, which is shorter than its diff:
```python
import functools

import jax
import jax.numpy as jnp
from jax import lax
from jax.experimental import pallas as pl
from jax.experimental.pallas import tpu as pltpu
from jax.sharding import Mesh
from jax.sharding import PartitionSpec as P

BLK = ("blk_0", "blk_1", "blk_2")
GRP = ("grp_0", "grp_1")
BLK_GRP = BLK + GRP
WIDTH = 2048
f32, bf16 = jnp.float32, jnp.bfloat16
VMEM = pl.BlockSpec(memory_space=pltpu.VMEM)


def halves(value):
    high = value.astype(bf16)
    return high, (value - high.astype(f32)).astype(bf16)


def stacked_halves(value):
    return jnp.concatenate(halves(value), axis=0)


def fold(both):
    half = both.shape[0] // 2
    return both[:half] + both[half:]


def dot_rows(probes_hl, high, low):
    dims = (((1,), (1,)), ((), ()))
    return fold(
        lax.dot_general(probes_hl, high, dims, preferred_element_type=f32)
        + lax.dot_general(probes_hl, low, dims, preferred_element_type=f32)
    )


def dot_columns(slab_hl, high, low):
    return fold(
        jnp.dot(slab_hl, high, preferred_element_type=f32)
        + jnp.dot(slab_hl, low, preferred_element_type=f32)
    )


def offsets(rows, cols):
    return lax.axis_index(GRP) * rows, lax.axis_index(BLK) * cols


def ids(shape, row0, col0):
    return (
        row0 + lax.broadcasted_iota(jnp.int32, shape, 0),
        col0 + lax.broadcasted_iota(jnp.int32, shape, 1),
    )


def row_kernel(cols, sat, ter, probes, out, high_out, low_out):
    step = pl.program_id(0)
    rows = sat.shape[0]
    n = probes.shape[0]
    row0, dev_col0 = offsets(rows, cols)
    col0 = dev_col0 + step * WIDTH

    @pl.when(step == 0)
    def _():
        out[...] = jnp.zeros_like(out)

    probes_hl = stacked_halves(probes[...])
    here = pl.ds(pl.multiple_of(step * WIDTH, WIDTH), WIDTH)
    crossed = col0 < row0 + rows

    def products(masked):
        for k, matrix in enumerate((sat, ter)):
            block = matrix[...]
            if masked:
                r, c = ids(block.shape, row0, col0)
                block = jnp.where(c > r, block, 0.0)
            high, low = halves(block)
            high_out[k, :, here] = high
            low_out[k, :, here] = low
            out[k * n : (k + 1) * n] += dot_rows(probes_hl, high, low)

    @pl.when(jnp.logical_not(crossed))
    def _():
        products(False)

    @pl.when(crossed)
    def _():
        products(True)

    @pl.when((row0 >= col0) & (row0 < col0 + WIDTH))
    def _():
        at = pl.ds(pl.multiple_of(row0 - col0, rows), rows)
        slab = probes[:, at]
        out[2 * n : 3 * n] = slab
        r, c = ids((rows, rows), 0, 0)
        for k, matrix in enumerate((sat, ter)):
            diagonal = jnp.sum(jnp.where(r == c, matrix[:, at], 0.0), axis=0, keepdims=True)
            out[3 * n + k : 3 * n + k + 1] = diagonal
            out[k * n : (k + 1) * n] += diagonal * slab


def row_products(sat, ter, probes):
    rows, cols = sat.shape
    n = probes.shape[0]
    return pl.pallas_call(
        functools.partial(row_kernel, cols),
        grid=(cols // WIDTH,),
        in_specs=[
            pl.BlockSpec((rows, WIDTH), lambda j: (0, j)),
            pl.BlockSpec((rows, WIDTH), lambda j: (0, j)),
            pl.BlockSpec((n, WIDTH), lambda j: (0, j)),
        ],
        out_specs=[VMEM] * 3,
        out_shape=[jax.ShapeDtypeStruct((3 * n + 8, rows), f32)]
        + [jax.ShapeDtypeStruct((2, rows, cols), bf16)] * 2,
        compiler_params=pltpu.CompilerParams(vmem_limit_bytes=44 * 2**20),
        name="row_products",
    )(sat, ter, probes)


def column_kernel(cols, n, parts, high, low, held, arrived, out, row_part):
    shared = held[...] + arrived[...]
    slab = shared[2 * n : 3 * n]
    slab_hl = stacked_halves(slab)
    width = cols // parts
    groups = width // 128
    for part in range(parts):
        at = slice(part * width, (part + 1) * width)
        for k in range(2):
            result = dot_columns(slab_hl, high[k, :, at], low[k, :, at])
            for q in range(groups):
                to = q * 2 * n + k * n
                out[part, to : to + n] = result[:, q * 128 : (q + 1) * 128]

    eye = jnp.equal(*ids((n, 128), 0, 0))
    tail = []
    for k in range(2):
        direct = shared[k * n : (k + 1) * n]
        row_part[k] = direct
        diagonal = shared[3 * n + k : 3 * n + k + 1]
        term = jnp.sum(slab * (2.0 * direct - diagonal * slab), axis=1, keepdims=True)
        tail.append(jnp.sum(jnp.where(eye, term, 0.0), axis=0, keepdims=True))
    tail.append(jnp.zeros((6, 128), f32))
    tail = jnp.concatenate(tail, axis=0)
    for part in range(parts):
        out[part, groups * 2 * n : groups * 2 * n + 8] = tail


def column_products(high, low, held, arrived, n, parts):
    _, rows, cols = high.shape
    chunk = (cols // parts // 128) * 2 * n + 8
    return pl.pallas_call(
        functools.partial(column_kernel, cols, n, parts),
        in_specs=[VMEM] * 4,
        out_specs=[VMEM] * 2,
        out_shape=[
            jax.ShapeDtypeStruct((parts, chunk, 128), f32),
            jax.ShapeDtypeStruct((2, n, rows), f32),
        ],
        compiler_params=pltpu.CompilerParams(vmem_limit_bytes=24 * 2**20),
        name="column_products",
    )(high, low, held, arrived)


def sum_kernel(n, arrived, column_part, trace):
    parts, chunk, _ = arrived.shape
    groups = (chunk - 8) // (2 * n)
    total = arrived[0]
    for part in range(1, parts):
        total = total + arrived[part]
    for q in range(groups):
        for k in range(2):
            at = q * 2 * n + k * n
            column_part[k, :, q * 128 : (q + 1) * 128] = total[at : at + n]
    trace[...] = total[groups * 2 * n : groups * 2 * n + 2, :n]


def sum_parts(arrived, n, width):
    return pl.pallas_call(
        functools.partial(sum_kernel, n),
        in_specs=[VMEM],
        out_specs=[VMEM, VMEM],
        out_shape=[
            jax.ShapeDtypeStruct((2, n, width), f32),
            jax.ShapeDtypeStruct((2, n), f32),
        ],
        compiler_params=pltpu.CompilerParams(vmem_limit_bytes=8 * 2**20),
        name="sum_parts",
    )(arrived)


def add_kernel(*refs):
    *terms, out = refs
    sums = [ref[...] for ref in terms]
    while len(sums) > 1:
        sums = [a + b for a, b in zip(sums[::2], sums[1::2], strict=True)]
    out[...] = sums[0]


def added(*terms):
    return pl.pallas_call(
        add_kernel,
        in_specs=[VMEM] * len(terms),
        out_specs=VMEM,
        out_shape=jax.ShapeDtypeStruct(terms[0].shape, f32),
        compiler_params=pltpu.CompilerParams(vmem_limit_bytes=2 * 2**20),
        name="added",
    )(*terms)


def exchanged(value, bits):
    size = lax.axis_size(BLK)
    return lax.ppermute(value, BLK, [(i, i ^ bits) for i in range(size)])


def summed_over_four(value, first, second):
    a, b, c = (exchanged(value, bits) for bits in (first, second, first ^ second))
    return added(value, a, b, c)


def shards(matrix_sat, matrix_ter, probes):
    n, cols = probes.shape
    core, z1, z2, z4, y = 1, 2, 4, 8, 16
    shared, high, low = row_products(matrix_sat, matrix_ter, probes)
    shared = added(shared, exchanged(shared, core))
    shared = summed_over_four(shared, y, z1)
    shared = added(shared, exchanged(shared, z2))
    arrived = exchanged(shared, z4)
    parts = lax.axis_size(GRP)
    mirrored, row_part = column_products(
        high, low, shared, arrived, n, parts
    )
    arrived = lax.all_to_all(mirrored, GRP, split_axis=0, concat_axis=0, tiled=True)
    column_part, trace_terms = sum_parts(arrived, n, cols // parts)
    return row_part, column_part, trace_terms


def solution(mesh):
    split = Mesh(mesh.devices.reshape(2, 8, 2, 2, 4), BLK_GRP)
    in_specs = (P(GRP, BLK), P(GRP, BLK), P(None, BLK))
    out_specs = (P(None, None, GRP), P(None, None, BLK_GRP), P())
    return jax.shard_map(
        shards, mesh=split, in_specs=in_specs, out_specs=out_specs, check_vma=False
    )
```

time: 58.5 us -> 49.6 us (0.85)
  Pallas kernels: 13.9 us -> 8.01 us
  waiting for transfers between devices: 11.2 us -> 9.32 us
  other arithmetic: 1.48 us -> 0 us
  local copies, waits for them, and re-layouts: 0 us -> 0.94 us
  blocking collectives: 16.9 us -> 16.2 us
    pallas_call x1 -> x4, Pallas kernels: 5.99 us -> 1.96 us  [the longest x1 1.93 us: column_products(): pl.pallas_call(functools.partial(column_kernel, cols, n, parts), in_specs...]
    ppermute x5 -> x6, waiting for transfers between devices: 11.2 us -> 9.32 us  [exchanged(): return lax.ppermute(value, BLK, [(i, i ^ bits) for i in range(size)])]
    add x5 -> x0, other arithmetic: 1.48 us -> none  [exchanged_sum(): value + lax.ppermute(value, axis, [(i, i ^ bit) for i in range(size)])]
    pallas_call x1, Pallas kernels: 1.71 us -> 0.66 us  [sum_parts(): pl.pallas_call(functools.partial(sum_kernel, n), in_specs=[VMEM], out_spe...]
    unnamed x0 -> x2, local copies, waits for them, and re-layouts: none -> 0.94 us
    pallas_call x1, Pallas kernels: 6.21 us -> 5.39 us  [row_products(): pl.pallas_call(functools.partial(row_kernel, cols), grid=(cols // WIDTH,)...]
    all_to_all x1, blocking collectives: 16.9 us -> 16.2 us  [shards(): lax.all_to_all(mirrored, GRP, split_axis=0, concat_axis=0, tiled=True)]
    ppermute x5 -> x6, starting transfers between devices: 14.1 us -> 14.3 us  [exchanged(): return lax.ppermute(value, BLK, [(i, i ^ bits) for i in range(size)])]
  transfers between devices with their start and end apart: 5 -> 6, of which waited for: 5 -> 6; matrix products, arithmetic and copies ran while one was open for 0% -> 0% of each run, Pallas kernels for 0% -> 0%
where the time goes in v2:
time: 49.6 us; the launch traced here: 49.5 us
  blocking collectives  16.2 us (33%)
  starting transfers between devices  14.3 us (29%)
  waiting for transfers between devices  9.32 us (19%)
  Pallas kernels  8.01 us (16%)
  local copies, waits for them, and re-layouts  0.94 us (2%)
  between operations  0.66 us (1%)
    all_to_all x1, blocking collectives, shards(): lax.all_to_all(mirrored, GRP, split_axis=0, concat_axis=0, tiled=True)  16.2 us
    ppermute x6, starting transfers between devices, exchanged(): return lax.ppermute(value, BLK, [(i, i ^ bits) for i in range(size)])  14.3 us
    ppermute x6, waiting for transfers between devices, exchanged(): return lax.ppermute(value, BLK, [(i, i ^ bits) for i in range(size)])  9.32 us
    pallas_call x1, Pallas kernels, row_products(): pl.pallas_call(functools.partial(row_kernel, cols), grid=(cols // WIDTH,)...  5.39 us
    pallas_call x1, Pallas kernels, column_products(): pl.pallas_call(functools.partial(column_kernel, cols, n, parts), in_specs...  1.93 us
  transfers between devices with their start and end apart: 6, of which 6 were waited for; matrix products, arithmetic and copies ran while one was open for 0% of the time, Pallas kernels for 0%

profile of v2, /device:TPU:2, one launch (start us, length us, event | category | flops | bytes accessed | tf_op | source)
XLA Modules:
  0.0 49.5 jit_solution(2057162685959572506)
XLA Ops:
  0.6 0.0 copy-start
  0.6 0.9 %copy-done = f32[16,4096]{1,0:T(8,128)S(1)} copy-done((f32[16,4096]{1,0:T(8,128)S(1)}, f32[16,4096]{1,0:T(8,128)}, u32[]{:S(2)}) %copy-start) | copy-done | bytes 262168
  1.6 5.4 %row_products.1 = (f32[56,256]{1,0:T(8,128)S(1)}, bf16[2,256,4096]{2,1,0:T(8,128)(2,1)S(1)}, bf16[2,256,4096]{2,1,0:T(8,128)(2,1)S(1)}) custom-call(f32[256,4096]{1,0:T(8,128)} %sat.1, f32[256,4096]{1,0:T(8,128)} %ter.1, f32[16,4096]{1,0:T(8,128)S(1)} %copy-done), custom_call_target="tpu_custom_call" | custom-call | tf_op jit(solution)/shard_map/row_products/pallas_call | solution.py:108
  7.0 0.0 collective-permute-start
  7.0 1.2 %collective-permute-done.refs_1_ = f32[56,256]{1,0:T(8,128)S(1)} collective-permute-done((f32[56,256]{1,0:T(8,128)S(1)}, f32[56,256]{1,0:T(8,128)S(1)}, u32[]{:S(2)}, u32[]{:S(2)}) %collective-permute-start) | collective-permute-done | bytes 57376 | tf_op jit(solution)/shard_map/ppermute | solution.py:216
  8.3 2.9 %collective-permute-start.3 = (f32[56,256]{1,0:T(8,128)S(1)}, f32[56,256]{1,0:T(8,128)S(1)}, u32[]{:S(2)}, u32[]{:S(2)}) collective-permute-start(f32[56,256]{1,0:T(8,128)S(1)} %added.3.refs_0_), channel_id=1, source_target_pairs={{0,144},{8,152},{16,128},{24,136},{32,176},{40,184},{48,160},{56,1... | collective-permute-start | bytes 172040 | tf_op jit(solution)/shard_map/ppermute | solution.py:216
  11.1 0.1 collective-permute-start.2
  11.2 0.6 %collective-permute-start.1 = (f32[56,256]{1,0:T(8,128)S(1)}, f32[56,256]{1,0:T(8,128)S(1)}, u32[]{:S(2)}, u32[]{:S(2)}) collective-permute-start(f32[56,256]{1,0:T(8,128)S(1)} %added.3.refs_0_), channel_id=1, source_target_pairs={{0,128},{8,136},{16,144},{24,152},{32,160},{40,168},{48,176},{56,1... | collective-permute-start | bytes 172040 | tf_op jit(solution)/shard_map/ppermute | solution.py:216
  11.8 1.6 %collective-permute-done.3.refs_3_ = f32[56,256]{1,0:T(8,128)S(1)} collective-permute-done((f32[56,256]{1,0:T(8,128)S(1)}, f32[56,256]{1,0:T(8,128)S(1)}, u32[]{:S(2)}, u32[]{:S(2)}) %collective-permute-start.3) | collective-permute-done | bytes 57376 | tf_op jit(solution)/shard_map/ppermute | solution.py:216
  13.4 1.9 %collective-permute-done.2.refs_2_ = f32[56,256]{1,0:T(8,128)S(1)} collective-permute-done((f32[56,256]{1,0:T(8,128)S(1)}, f32[56,256]{1,0:T(8,128)S(1)}, u32[]{:S(2)}, u32[]{:S(2)}) %collective-permute-start.2) | collective-permute-done | bytes 57376 | tf_op jit(solution)/shard_map/ppermute | solution.py:216
  15.3 0.1 collective-permute-done.1.refs_1_
  15.4 3.4 %collective-permute-start.4 = (f32[56,256]{1,0:T(8,128)S(1)}, f32[56,256]{1,0:T(8,128)S(1)}, u32[]{:S(2)}, u32[]{:S(2)}) collective-permute-start(f32[56,256]{1,0:T(8,128)S(1)} %added.4.refs_0_), channel_id=1, source_target_pairs={{0,32},{8,40},{16,48},{24,56},{32,0},{40,8},{48,16},{56,24},{64,96... | collective-permute-start | bytes 172040 | tf_op jit(solution)/shard_map/ppermute | solution.py:216
  18.8 2.4 %collective-permute-done.4.refs_1_ = f32[56,256]{1,0:T(8,128)S(1)} collective-permute-done((f32[56,256]{1,0:T(8,128)S(1)}, f32[56,256]{1,0:T(8,128)S(1)}, u32[]{:S(2)}, u32[]{:S(2)}) %collective-permute-start.4) | collective-permute-done | bytes 57376 | tf_op jit(solution)/shard_map/ppermute | solution.py:216
  21.2 7.3 %collective-permute-start.5 = (f32[56,256]{1,0:T(8,128)S(1)}, f32[56,256]{1,0:T(8,128)S(1)}, u32[]{:S(2)}, u32[]{:S(2)}) collective-permute-start(f32[56,256]{1,0:T(8,128)S(1)} %added.5.held), channel_id=1, source_target_pairs={{0,64},{8,72},{16,80},{24,88},{32,96},{40,104},{48,112},{56,120},{... | collective-permute-start | bytes 172040 | tf_op jit(solution)/shard_map/ppermute | solution.py:216
  28.5 2.2 %collective-permute-done.5.arrived = f32[56,256]{1,0:T(8,128)S(1)} collective-permute-done((f32[56,256]{1,0:T(8,128)S(1)}, f32[56,256]{1,0:T(8,128)S(1)}, u32[]{:S(2)}, u32[]{:S(2)}) %collective-permute-start.5) | collective-permute-done | bytes 57376 | tf_op jit(solution)/shard_map/ppermute | solution.py:216
  30.7 1.9 %column_products.1 = (f32[8,136,128]{2,1,0:T(8,128)S(1)}, f32[2,16,256]{2,1,0:T(8,128)}) custom-call(bf16[2,256,4096]{2,1,0:T(8,128)(2,1)S(1)} %get-tuple-element.10.high, bf16[2,256,4096]{2,1,0:T(8,128)(2,1)S(1)} %get-tuple-element.11.low, f32[56,256]{1,0:T(8,128)S(1)} %added.5.held, f32[56,256]{1,0:T(8,128)S(1)} %collective-permute-done.5.arrived), custom_call_target="tpu_custom_call" | custom-call | tf_op jit(solution)/shard_map/column_products/pallas_call | solution.py:155
  32.6 16.2 %all_to_all.5.arrived = f32[8,136,128]{2,1,0:T(8,128)S(1)} all-to-all(f32[8,136,128]{2,1,0:T(8,128)S(1)} %get-tuple-element.14), channel_id=1, replica_groups=mesh['blk_0'=2,'blk_1'=8,'blk_2'=2,'grp_0'=2,'grp_1'=4] {'grp_0','grp_1'}, dimensions={0} | all-to-all | bytes 1114112 | tf_op jit(solution)/shard_map/all_to_all | solution.py:236
  48.8 0.7 %sum_parts.1 = (f32[2,16,512]{2,1,0:T(8,128)}, f32[2,16]{1,0:T(2,128)}) custom-call(f32[8,136,128]{2,1,0:T(8,128)S(1)} %all_to_all.5.arrived), custom_call_target="tpu_custom_call" | custom-call | tf_op jit(solution)/shard_map/sum_parts/pallas_call | solution.py:182
  (3 shorter events, 0.0 us)
Async XLA Ops:
  0.6 1.0 %copy-start = (f32[16,4096]{1,0:T(8,128)S(1)}, f32[16,4096]{1,0:T(8,128)}, u32[]{:S(2)}) copy-start(f32[16,4096]{1,0:T(8,128)} %probes.1) | copy-start | bytes 786436
  7.0 1.3 %collective-permute-start = (f32[56,256]{1,0:T(8,128)S(1)}, f32[56,256]{1,0:T(8,128)S(1)}, u32[]{:S(2)}, u32[]{:S(2)}) collective-permute-start(f32[56,256]{1,0:T(8,128)S(1)} %get-tuple-element.12.refs_0_), channel_id=1, source_target_pairs={{0,8},{8,0},{16,24},{24,16},{32,40},{40,32},{48,56},{56,48},{64,72... | collective-permute-start | bytes 172040 | tf_op jit(solution)/shard_map/ppermute | solution.py:216
  8.3 5.2 %collective-permute-start.3 = (f32[56,256]{1,0:T(8,128)S(1)}, f32[56,256]{1,0:T(8,128)S(1)}, u32[]{:S(2)}, u32[]{:S(2)}) collective-permute-start(f32[56,256]{1,0:T(8,128)S(1)} %added.3.refs_0_), channel_id=1, source_target_pairs={{0,144},{8,152},{16,128},{24,136},{32,176},{40,184},{48,160},{56,1... | collective-permute-start | bytes 172040 | tf_op jit(solution)/shard_map/ppermute | solution.py:216
  11.1 4.2 %collective-permute-start.2 = (f32[56,256]{1,0:T(8,128)S(1)}, f32[56,256]{1,0:T(8,128)S(1)}, u32[]{:S(2)}, u32[]{:S(2)}) collective-permute-start(f32[56,256]{1,0:T(8,128)S(1)} %added.3.refs_0_), channel_id=1, source_target_pairs={{0,16},{8,24},{16,0},{24,8},{32,48},{40,56},{48,32},{56,40},{64,80... | collective-permute-start | bytes 172040 | tf_op jit(solution)/shard_map/ppermute | solution.py:216
  11.2 4.2 %collective-permute-start.1 = (f32[56,256]{1,0:T(8,128)S(1)}, f32[56,256]{1,0:T(8,128)S(1)}, u32[]{:S(2)}, u32[]{:S(2)}) collective-permute-start(f32[56,256]{1,0:T(8,128)S(1)} %added.3.refs_0_), channel_id=1, source_target_pairs={{0,128},{8,136},{16,144},{24,152},{32,160},{40,168},{48,176},{56,1... | collective-permute-start | bytes 172040 | tf_op jit(solution)/shard_map/ppermute | solution.py:216
  15.4 5.7 %collective-permute-start.4 = (f32[56,256]{1,0:T(8,128)S(1)}, f32[56,256]{1,0:T(8,128)S(1)}, u32[]{:S(2)}, u32[]{:S(2)}) collective-permute-start(f32[56,256]{1,0:T(8,128)S(1)} %added.4.refs_0_), channel_id=1, source_target_pairs={{0,32},{8,40},{16,48},{24,56},{32,0},{40,8},{48,16},{56,24},{64,96... | collective-permute-start | bytes 172040 | tf_op jit(solution)/shard_map/ppermute | solution.py:216
  21.2 9.5 %collective-permute-start.5 = (f32[56,256]{1,0:T(8,128)S(1)}, f32[56,256]{1,0:T(8,128)S(1)}, u32[]{:S(2)}, u32[]{:S(2)}) collective-permute-start(f32[56,256]{1,0:T(8,128)S(1)} %added.5.held), channel_id=1, source_target_pairs={{0,64},{8,72},{16,80},{24,88},{32,96},{40,104},{48,112},{56,120},{... | collective-permute-start | bytes 172040 | tf_op jit(solution)/shard_map/ppermute | solution.py:216

commit v3 on v2

--- a/solution.py
+++ b/solution.py
@@ -16,6 +16,10 @@
 VMEM = pl.BlockSpec(memory_space=pltpu.VMEM)
 
 
+def in_hbm(value):
+    return pltpu.with_memory_space_constraint(value, pltpu.HBM)
+
+
 def halves(value):
     high = value.astype(bf16)
     return high, (value - high.astype(f32)).astype(bf16)
@@ -34,7 +38,7 @@
     dims = (((1,), (1,)), ((), ()))
     return fold(
         lax.dot_general(probes_hl, high, dims, preferred_element_type=f32)
-        + lax.dot_general(probes_hl, low, dims, preferred_element_type=f32)
+        + lax.dot_general(low, probes_hl, dims, preferred_element_type=f32).T
     )
 
 
@@ -53,6 +57,18 @@
     return (
         row0 + lax.broadcasted_iota(jnp.int32, shape, 0),
         col0 + lax.broadcasted_iota(jnp.int32, shape, 1),
+    )
+
+
+def put(ref, start, stride, value):
+    size, lanes = value.shape
+    for q in range(lanes // 128):
+        ref[start + q * stride : start + q * stride + size] = value[:, q * 128 : (q + 1) * 128]
+
+
+def take(ref, start, size, stride, lanes):
+    return jnp.concatenate(
+        [ref[start + q * stride : start + q * stride + size] for q in range(lanes // 128)], axis=1
     )
 
 
@@ -80,7 +96,8 @@
             high, low = halves(block)
             high_out[k, :, here] = high
             low_out[k, :, here] = low
-            out[k * n : (k + 1) * n] += dot_rows(probes_hl, high, low)
+            sums = take(out, k * n, n, 2 * n, rows) + dot_rows(probes_hl, high, low)
+            put(out, k * n, 2 * n, sums)
 
     @pl.when(jnp.logical_not(crossed))
     def _():
@@ -94,12 +111,12 @@
     def _():
         at = pl.ds(pl.multiple_of(row0 - col0, rows), rows)
         slab = probes[:, at]
-        out[2 * n : 3 * n] = slab
+        put(out, 4 * n, n, slab)
         r, c = ids((rows, rows), 0, 0)
         for k, matrix in enumerate((sat, ter)):
             diagonal = jnp.sum(jnp.where(r == c, matrix[:, at], 0.0), axis=0, keepdims=True)
-            out[3 * n + k : 3 * n + k + 1] = diagonal
-            out[k * n : (k + 1) * n] += diagonal * slab
+            put(out, 6 * n + k, 2, diagonal)
+            put(out, k * n, 2 * n, take(out, k * n, n, 2 * n, rows) + diagonal * slab)
 
 
 def row_products(sat, ter, probes):
@@ -114,16 +131,17 @@
             pl.BlockSpec((n, WIDTH), lambda j: (0, j)),
         ],
         out_specs=[VMEM] * 3,
-        out_shape=[jax.ShapeDtypeStruct((3 * n + 8, rows), f32)]
+        out_shape=[jax.ShapeDtypeStruct((3 * n * (rows // 128) + 8, 128), f32)]
         + [jax.ShapeDtypeStruct((2, rows, cols), bf16)] * 2,
         compiler_params=pltpu.CompilerParams(vmem_limit_bytes=44 * 2**20),
         name="row_products",
-    )(sat, ter, probes)
+    )(in_hbm(sat), in_hbm(ter), in_hbm(probes))
 
 
 def column_kernel(cols, n, parts, high, low, held, arrived, out, row_part):
     shared = held[...] + arrived[...]
-    slab = shared[2 * n : 3 * n]
+    rows = row_part.shape[2]
+    slab = take(shared, 4 * n, n, n, rows)
     slab_hl = stacked_halves(slab)
     width = cols // parts
     groups = width // 128
@@ -138,9 +156,9 @@
     eye = jnp.equal(*ids((n, 128), 0, 0))
     tail = []
     for k in range(2):
-        direct = shared[k * n : (k + 1) * n]
+        direct = take(shared, k * n, n, 2 * n, rows)
         row_part[k] = direct
-        diagonal = shared[3 * n + k : 3 * n + k + 1]
+        diagonal = take(shared, 6 * n + k, 1, 2, rows)
         term = jnp.sum(slab * (2.0 * direct - diagonal * slab), axis=1, keepdims=True)
         tail.append(jnp.sum(jnp.where(eye, term, 0.0), axis=0, keepdims=True))
     tail.append(jnp.zeros((6, 128), f32))

time: 49.6 us -> 48.1 us (0.970)
  local copies, waits for them, and re-layouts: 0.94 us -> 0 us
    unnamed x2 -> x0, local copies, waits for them, and re-layouts: 0.94 us -> none
where the time goes in v3:
time: 48.1 us; the launch traced here: 48 us
  blocking collectives  16.2 us (34%)
  starting transfers between devices  14.5 us (30%)
  waiting for transfers between devices  9.02 us (19%)
  Pallas kernels  7.66 us (16%)
  between operations  0.66 us (1%)
    all_to_all x1, blocking collectives, shards(): lax.all_to_all(mirrored, GRP, split_axis=0, concat_axis=0, tiled=True)  16.2 us
    ppermute x6, starting transfers between devices, exchanged(): return lax.ppermute(value, BLK, [(i, i ^ bits) for i in range(size)])  14.5 us
    ppermute x6, waiting for transfers between devices, exchanged(): return lax.ppermute(value, BLK, [(i, i ^ bits) for i in range(size)])  9.02 us
    pallas_call x1, Pallas kernels, row_products(): pl.pallas_call(functools.partial(row_kernel, cols), grid=(cols // WIDTH,)...  5.04 us
    pallas_call x1, Pallas kernels, column_products(): pl.pallas_call(functools.partial(column_kernel, cols, n, parts), in_specs...  1.93 us
  transfers between devices with their start and end apart: 6, of which 6 were waited for; matrix products, arithmetic and copies ran while one was open for 0% of the time, Pallas kernels for 0%

profile of v3, /device:TPU:2, one launch (start us, length us, event | category | flops | bytes accessed | tf_op | source)
XLA Modules:
  0.0 48.0 jit_solution(10773436110957483497)
XLA Ops:
  0.6 5.0 %row_products.1 = (f32[104,128]{1,0:T(8,128)S(1)}, bf16[2,256,4096]{2,1,0:T(8,128)(2,1)S(1)}, bf16[2,256,4096]{2,1,0:T(8,128)(2,1)S(1)}) custom-call(f32[256,4096]{1,0:T(8,128)} %sat.1, f32[256,4096]{1,0:T(8,128)} %ter.1, f32[16,4096]{1,0:T(8,128)} %probes.1), custom_call_target="tpu_custom_call" | custom-call | tf_op jit(solution)/shard_map/row_products/pallas_call | solution.py:125
  5.7 0.1 collective-permute-start
  5.8 1.2 %collective-permute-done.refs_1_ = f32[104,128]{1,0:T(8,128)S(1)} collective-permute-done((f32[104,128]{1,0:T(8,128)S(1)}, f32[104,128]{1,0:T(8,128)S(1)}, u32[]{:S(2)}, u32[]{:S(2)}) %collective-permute-start) | collective-permute-done | bytes 53280 | tf_op jit(solution)/shard_map/ppermute | solution.py:234
  7.0 2.8 %collective-permute-start.3 = (f32[104,128]{1,0:T(8,128)S(1)}, f32[104,128]{1,0:T(8,128)S(1)}, u32[]{:S(2)}, u32[]{:S(2)}) collective-permute-start(f32[104,128]{1,0:T(8,128)S(1)} %added.3.refs_0_), channel_id=1, source_target_pairs={{0,144},{8,152},{16,128},{24,136},{32,176},{40,184},{48,160},{56,1... | collective-permute-start | bytes 159752 | tf_op jit(solution)/shard_map/ppermute | solution.py:234
  9.9 0.1 collective-permute-start.2
  10.0 0.6 %collective-permute-start.1 = (f32[104,128]{1,0:T(8,128)S(1)}, f32[104,128]{1,0:T(8,128)S(1)}, u32[]{:S(2)}, u32[]{:S(2)}) collective-permute-start(f32[104,128]{1,0:T(8,128)S(1)} %added.3.refs_0_), channel_id=1, source_target_pairs={{0,128},{8,136},{16,144},{24,152},{32,160},{40,168},{48,176},{56,1... | collective-permute-start | bytes 159752 | tf_op jit(solution)/shard_map/ppermute | solution.py:234
  10.6 1.5 %collective-permute-done.3.refs_3_ = f32[104,128]{1,0:T(8,128)S(1)} collective-permute-done((f32[104,128]{1,0:T(8,128)S(1)}, f32[104,128]{1,0:T(8,128)S(1)}, u32[]{:S(2)}, u32[]{:S(2)}) %collective-permute-start.3) | collective-permute-done | bytes 53280 | tf_op jit(solution)/shard_map/ppermute | solution.py:234
  12.1 1.9 %collective-permute-done.2.refs_2_ = f32[104,128]{1,0:T(8,128)S(1)} collective-permute-done((f32[104,128]{1,0:T(8,128)S(1)}, f32[104,128]{1,0:T(8,128)S(1)}, u32[]{:S(2)}, u32[]{:S(2)}) %collective-permute-start.2) | collective-permute-done | bytes 53280 | tf_op jit(solution)/shard_map/ppermute | solution.py:234
  14.0 0.1 collective-permute-done.1.refs_1_
  14.1 3.4 %collective-permute-start.4 = (f32[104,128]{1,0:T(8,128)S(1)}, f32[104,128]{1,0:T(8,128)S(1)}, u32[]{:S(2)}, u32[]{:S(2)}) collective-permute-start(f32[104,128]{1,0:T(8,128)S(1)} %added.4.refs_0_), channel_id=1, source_target_pairs={{0,32},{8,40},{16,48},{24,56},{32,0},{40,8},{48,16},{56,24},{64,96... | collective-permute-start | bytes 159752 | tf_op jit(solution)/shard_map/ppermute | solution.py:234
  17.5 2.2 %collective-permute-done.4.refs_1_ = f32[104,128]{1,0:T(8,128)S(1)} collective-permute-done((f32[104,128]{1,0:T(8,128)S(1)}, f32[104,128]{1,0:T(8,128)S(1)}, u32[]{:S(2)}, u32[]{:S(2)}) %collective-permute-start.4) | collective-permute-done | bytes 53280 | tf_op jit(solution)/shard_map/ppermute | solution.py:234
  19.7 7.4 %collective-permute-start.5 = (f32[104,128]{1,0:T(8,128)S(1)}, f32[104,128]{1,0:T(8,128)S(1)}, u32[]{:S(2)}, u32[]{:S(2)}) collective-permute-start(f32[104,128]{1,0:T(8,128)S(1)} %added.5.held), channel_id=1, source_target_pairs={{0,64},{8,72},{16,80},{24,88},{32,96},{40,104},{48,112},{56,120},{... | collective-permute-start | bytes 159752 | tf_op jit(solution)/shard_map/ppermute | solution.py:234
  27.1 2.1 %collective-permute-done.5.arrived = f32[104,128]{1,0:T(8,128)S(1)} collective-permute-done((f32[104,128]{1,0:T(8,128)S(1)}, f32[104,128]{1,0:T(8,128)S(1)}, u32[]{:S(2)}, u32[]{:S(2)}) %collective-permute-start.5) | collective-permute-done | bytes 53280 | tf_op jit(solution)/shard_map/ppermute | solution.py:234
  29.2 1.9 %column_products.1 = (f32[8,136,128]{2,1,0:T(8,128)S(1)}, f32[2,16,256]{2,1,0:T(8,128)}) custom-call(bf16[2,256,4096]{2,1,0:T(8,128)(2,1)S(1)} %get-tuple-element.10.high, bf16[2,256,4096]{2,1,0:T(8,128)(2,1)S(1)} %get-tuple-element.11.low, f32[104,128]{1,0:T(8,128)S(1)} %added.5.held, f32[104,128]{1,0:T(8,128)S(1)} %collective-permute-done.5.arrived), custom_call_target="tpu_custom_call" | custom-call | tf_op jit(solution)/shard_map/column_products/pallas_call | solution.py:173
  31.1 16.2 %all_to_all.5.arrived = f32[8,136,128]{2,1,0:T(8,128)S(1)} all-to-all(f32[8,136,128]{2,1,0:T(8,128)S(1)} %get-tuple-element.14), channel_id=1, replica_groups=mesh['blk_0'=2,'blk_1'=8,'blk_2'=2,'grp_0'=2,'grp_1'=4] {'grp_0','grp_1'}, dimensions={0} | all-to-all | bytes 1114112 | tf_op jit(solution)/shard_map/all_to_all | solution.py:254
  47.3 0.7 %sum_parts.1 = (f32[2,16,512]{2,1,0:T(8,128)}, f32[2,16]{1,0:T(2,128)}) custom-call(f32[8,136,128]{2,1,0:T(8,128)S(1)} %all_to_all.5.arrived), custom_call_target="tpu_custom_call" | custom-call | tf_op jit(solution)/shard_map/sum_parts/pallas_call | solution.py:200
  (3 shorter events, 0.0 us)
Async XLA Ops:
  5.7 1.3 %collective-permute-start = (f32[104,128]{1,0:T(8,128)S(1)}, f32[104,128]{1,0:T(8,128)S(1)}, u32[]{:S(2)}, u32[]{:S(2)}) collective-permute-start(f32[104,128]{1,0:T(8,128)S(1)} %get-tuple-element.12.refs_0_), channel_id=1, source_target_pairs={{0,8},{8,0},{16,24},{24,16},{32,40},{40,32},{48,56},{56,48},{64,72... | collective-permute-start | bytes 159752 | tf_op jit(solution)/shard_map/ppermute | solution.py:234
  7.0 5.1 %collective-permute-start.3 = (f32[104,128]{1,0:T(8,128)S(1)}, f32[104,128]{1,0:T(8,128)S(1)}, u32[]{:S(2)}, u32[]{:S(2)}) collective-permute-start(f32[104,128]{1,0:T(8,128)S(1)} %added.3.refs_0_), channel_id=1, source_target_pairs={{0,144},{8,152},{16,128},{24,136},{32,176},{40,184},{48,160},{56,1... | collective-permute-start | bytes 159752 | tf_op jit(solution)/shard_map/ppermute | solution.py:234
  9.9 4.1 %collective-permute-start.2 = (f32[104,128]{1,0:T(8,128)S(1)}, f32[104,128]{1,0:T(8,128)S(1)}, u32[]{:S(2)}, u32[]{:S(2)}) collective-permute-start(f32[104,128]{1,0:T(8,128)S(1)} %added.3.refs_0_), channel_id=1, source_target_pairs={{0,16},{8,24},{16,0},{24,8},{32,48},{40,56},{48,32},{56,40},{64,80... | collective-permute-start | bytes 159752 | tf_op jit(solution)/shard_map/ppermute | solution.py:234
  10.0 4.1 %collective-permute-start.1 = (f32[104,128]{1,0:T(8,128)S(1)}, f32[104,128]{1,0:T(8,128)S(1)}, u32[]{:S(2)}, u32[]{:S(2)}) collective-permute-start(f32[104,128]{1,0:T(8,128)S(1)} %added.3.refs_0_), channel_id=1, source_target_pairs={{0,128},{8,136},{16,144},{24,152},{32,160},{40,168},{48,176},{56,1... | collective-permute-start | bytes 159752 | tf_op jit(solution)/shard_map/ppermute | solution.py:234
  14.1 5.5 %collective-permute-start.4 = (f32[104,128]{1,0:T(8,128)S(1)}, f32[104,128]{1,0:T(8,128)S(1)}, u32[]{:S(2)}, u32[]{:S(2)}) collective-permute-start(f32[104,128]{1,0:T(8,128)S(1)} %added.4.refs_0_), channel_id=1, source_target_pairs={{0,32},{8,40},{16,48},{24,56},{32,0},{40,8},{48,16},{56,24},{64,96... | collective-permute-start | bytes 159752 | tf_op jit(solution)/shard_map/ppermute | solution.py:234
  19.7 9.5 %collective-permute-start.5 = (f32[104,128]{1,0:T(8,128)S(1)}, f32[104,128]{1,0:T(8,128)S(1)}, u32[]{:S(2)}, u32[]{:S(2)}) collective-permute-start(f32[104,128]{1,0:T(8,128)S(1)} %added.5.held), channel_id=1, source_target_pairs={{0,64},{8,72},{16,80},{24,88},{32,96},{40,104},{48,112},{56,120},{... | collective-permute-start | bytes 159752 | tf_op jit(solution)/shard_map/ppermute | solution.py:234

commit v4 on v3

--- a/solution.py
+++ b/solution.py
@@ -245,8 +245,8 @@
     shared, high, low = row_products(matrix_sat, matrix_ter, probes)
     shared = added(shared, exchanged(shared, core))
     shared = summed_over_four(shared, y, z1)
-    shared = added(shared, exchanged(shared, z2))
-    arrived = exchanged(shared, z4)
+    shared = added(shared, exchanged(shared, z4))
+    arrived = exchanged(shared, z2)
     parts = lax.axis_size(GRP)
     mirrored, row_part = column_products(
         high, low, shared, arrived, n, parts

time: 48.1 us -> 48 us (level)
  starting transfers between devices: 14.5 us -> 13.6 us
    ppermute x6, starting transfers between devices: 14.5 us -> 13.6 us  [exchanged(): return lax.ppermute(value, BLK, [(i, i ^ bits) for i in range(size)])]
where the time goes in v4:
time: 48 us; the launch traced here: 47.5 us
  blocking collectives  16.2 us (34%)
  starting transfers between devices  13.6 us (28%)
  waiting for transfers between devices  9.41 us (20%)
  Pallas kernels  7.66 us (16%)
  between operations  0.66 us (1%)
    all_to_all x1, blocking collectives, shards(): lax.all_to_all(mirrored, GRP, split_axis=0, concat_axis=0, tiled=True)  16.2 us
    ppermute x6, starting transfers between devices, exchanged(): return lax.ppermute(value, BLK, [(i, i ^ bits) for i in range(size)])  13.6 us
    ppermute x6, waiting for transfers between devices, exchanged(): return lax.ppermute(value, BLK, [(i, i ^ bits) for i in range(size)])  9.41 us
    pallas_call x1, Pallas kernels, row_products(): pl.pallas_call(functools.partial(row_kernel, cols), grid=(cols // WIDTH,)...  5.04 us
    pallas_call x1, Pallas kernels, column_products(): pl.pallas_call(functools.partial(column_kernel, cols, n, parts), in_specs...  1.93 us
  transfers between devices with their start and end apart: 6, of which 6 were waited for; matrix products, arithmetic and copies ran while one was open for 0% of the time, Pallas kernels for 0%

profile of v4, /device:TPU:2, one launch (start us, length us, event | category | flops | bytes accessed | tf_op | source)
XLA Modules:
  0.0 47.5 jit_solution(9803773989487948343)
XLA Ops:
  0.6 5.0 %row_products.1 = (f32[104,128]{1,0:T(8,128)S(1)}, bf16[2,256,4096]{2,1,0:T(8,128)(2,1)S(1)}, bf16[2,256,4096]{2,1,0:T(8,128)(2,1)S(1)}) custom-call(f32[256,4096]{1,0:T(8,128)} %sat.1, f32[256,4096]{1,0:T(8,128)} %ter.1, f32[16,4096]{1,0:T(8,128)} %probes.1), custom_call_target="tpu_custom_call" | custom-call | tf_op jit(solution)/shard_map/row_products/pallas_call | solution.py:125
  5.7 0.1 collective-permute-start
  5.8 1.2 %collective-permute-done.refs_1_ = f32[104,128]{1,0:T(8,128)S(1)} collective-permute-done((f32[104,128]{1,0:T(8,128)S(1)}, f32[104,128]{1,0:T(8,128)S(1)}, u32[]{:S(2)}, u32[]{:S(2)}) %collective-permute-start) | collective-permute-done | bytes 53280 | tf_op jit(solution)/shard_map/ppermute | solution.py:234
  7.0 2.8 %collective-permute-start.3 = (f32[104,128]{1,0:T(8,128)S(1)}, f32[104,128]{1,0:T(8,128)S(1)}, u32[]{:S(2)}, u32[]{:S(2)}) collective-permute-start(f32[104,128]{1,0:T(8,128)S(1)} %added.3.refs_0_), channel_id=1, source_target_pairs={{0,144},{8,152},{16,128},{24,136},{32,176},{40,184},{48,160},{56,1... | collective-permute-start | bytes 159752 | tf_op jit(solution)/shard_map/ppermute | solution.py:234
  9.9 0.1 collective-permute-start.2
  10.0 0.6 %collective-permute-start.1 = (f32[104,128]{1,0:T(8,128)S(1)}, f32[104,128]{1,0:T(8,128)S(1)}, u32[]{:S(2)}, u32[]{:S(2)}) collective-permute-start(f32[104,128]{1,0:T(8,128)S(1)} %added.3.refs_0_), channel_id=1, source_target_pairs={{0,128},{8,136},{16,144},{24,152},{32,160},{40,168},{48,176},{56,1... | collective-permute-start | bytes 159752 | tf_op jit(solution)/shard_map/ppermute | solution.py:234
  10.6 1.5 %collective-permute-done.3.refs_3_ = f32[104,128]{1,0:T(8,128)S(1)} collective-permute-done((f32[104,128]{1,0:T(8,128)S(1)}, f32[104,128]{1,0:T(8,128)S(1)}, u32[]{:S(2)}, u32[]{:S(2)}) %collective-permute-start.3) | collective-permute-done | bytes 53280 | tf_op jit(solution)/shard_map/ppermute | solution.py:234
  12.1 1.9 %collective-permute-done.2.refs_2_ = f32[104,128]{1,0:T(8,128)S(1)} collective-permute-done((f32[104,128]{1,0:T(8,128)S(1)}, f32[104,128]{1,0:T(8,128)S(1)}, u32[]{:S(2)}, u32[]{:S(2)}) %collective-permute-start.2) | collective-permute-done | bytes 53280 | tf_op jit(solution)/shard_map/ppermute | solution.py:234
  14.0 0.1 collective-permute-done.1.refs_1_
  14.1 7.3 %collective-permute-start.4 = (f32[104,128]{1,0:T(8,128)S(1)}, f32[104,128]{1,0:T(8,128)S(1)}, u32[]{:S(2)}, u32[]{:S(2)}) collective-permute-start(f32[104,128]{1,0:T(8,128)S(1)} %added.4.refs_0_), channel_id=1, source_target_pairs={{0,64},{8,72},{16,80},{24,88},{32,96},{40,104},{48,112},{56,120},{... | collective-permute-start | bytes 159752 | tf_op jit(solution)/shard_map/ppermute | solution.py:234
  21.4 2.2 %collective-permute-done.4.refs_1_ = f32[104,128]{1,0:T(8,128)S(1)} collective-permute-done((f32[104,128]{1,0:T(8,128)S(1)}, f32[104,128]{1,0:T(8,128)S(1)}, u32[]{:S(2)}, u32[]{:S(2)}) %collective-permute-start.4) | collective-permute-done | bytes 53280 | tf_op jit(solution)/shard_map/ppermute | solution.py:234
  23.6 2.7 %collective-permute-start.5 = (f32[104,128]{1,0:T(8,128)S(1)}, f32[104,128]{1,0:T(8,128)S(1)}, u32[]{:S(2)}, u32[]{:S(2)}) collective-permute-start(f32[104,128]{1,0:T(8,128)S(1)} %added.5.held), channel_id=1, source_target_pairs={{0,32},{8,40},{16,48},{24,56},{32,0},{40,8},{48,16},{56,24},{64,96... | collective-permute-start | bytes 159752 | tf_op jit(solution)/shard_map/ppermute | solution.py:234
  26.3 2.5 %collective-permute-done.5.arrived = f32[104,128]{1,0:T(8,128)S(1)} collective-permute-done((f32[104,128]{1,0:T(8,128)S(1)}, f32[104,128]{1,0:T(8,128)S(1)}, u32[]{:S(2)}, u32[]{:S(2)}) %collective-permute-start.5) | collective-permute-done | bytes 53280 | tf_op jit(solution)/shard_map/ppermute | solution.py:234
  28.7 1.9 %column_products.1 = (f32[8,136,128]{2,1,0:T(8,128)S(1)}, f32[2,16,256]{2,1,0:T(8,128)}) custom-call(bf16[2,256,4096]{2,1,0:T(8,128)(2,1)S(1)} %get-tuple-element.10.high, bf16[2,256,4096]{2,1,0:T(8,128)(2,1)S(1)} %get-tuple-element.11.low, f32[104,128]{1,0:T(8,128)S(1)} %added.5.held, f32[104,128]{1,0:T(8,128)S(1)} %collective-permute-done.5.arrived), custom_call_target="tpu_custom_call" | custom-call | tf_op jit(solution)/shard_map/column_products/pallas_call | solution.py:173
  30.7 16.2 %all_to_all.5.arrived = f32[8,136,128]{2,1,0:T(8,128)S(1)} all-to-all(f32[8,136,128]{2,1,0:T(8,128)S(1)} %get-tuple-element.14), channel_id=1, replica_groups=mesh['blk_0'=2,'blk_1'=8,'blk_2'=2,'grp_0'=2,'grp_1'=4] {'grp_0','grp_1'}, dimensions={0} | all-to-all | bytes 1114112 | tf_op jit(solution)/shard_map/all_to_all | solution.py:254
  46.8 0.7 %sum_parts.1 = (f32[2,16,512]{2,1,0:T(8,128)}, f32[2,16]{1,0:T(2,128)}) custom-call(f32[8,136,128]{2,1,0:T(8,128)S(1)} %all_to_all.5.arrived), custom_call_target="tpu_custom_call" | custom-call | tf_op jit(solution)/shard_map/sum_parts/pallas_call | solution.py:200
  (3 shorter events, 0.0 us)
Async XLA Ops:
  5.7 1.3 %collective-permute-start = (f32[104,128]{1,0:T(8,128)S(1)}, f32[104,128]{1,0:T(8,128)S(1)}, u32[]{:S(2)}, u32[]{:S(2)}) collective-permute-start(f32[104,128]{1,0:T(8,128)S(1)} %get-tuple-element.12.refs_0_), channel_id=1, source_target_pairs={{0,8},{8,0},{16,24},{24,16},{32,40},{40,32},{48,56},{56,48},{64,72... | collective-permute-start | bytes 159752 | tf_op jit(solution)/shard_map/ppermute | solution.py:234
  7.0 5.1 %collective-permute-start.3 = (f32[104,128]{1,0:T(8,128)S(1)}, f32[104,128]{1,0:T(8,128)S(1)}, u32[]{:S(2)}, u32[]{:S(2)}) collective-permute-start(f32[104,128]{1,0:T(8,128)S(1)} %added.3.refs_0_), channel_id=1, source_target_pairs={{0,144},{8,152},{16,128},{24,136},{32,176},{40,184},{48,160},{56,1... | collective-permute-start | bytes 159752 | tf_op jit(solution)/shard_map/ppermute | solution.py:234
  9.9 4.1 %collective-permute-start.2 = (f32[104,128]{1,0:T(8,128)S(1)}, f32[104,128]{1,0:T(8,128)S(1)}, u32[]{:S(2)}, u32[]{:S(2)}) collective-permute-start(f32[104,128]{1,0:T(8,128)S(1)} %added.3.refs_0_), channel_id=1, source_target_pairs={{0,16},{8,24},{16,0},{24,8},{32,48},{40,56},{48,32},{56,40},{64,80... | collective-permute-start | bytes 159752 | tf_op jit(solution)/shard_map/ppermute | solution.py:234
  10.0 4.1 %collective-permute-start.1 = (f32[104,128]{1,0:T(8,128)S(1)}, f32[104,128]{1,0:T(8,128)S(1)}, u32[]{:S(2)}, u32[]{:S(2)}) collective-permute-start(f32[104,128]{1,0:T(8,128)S(1)} %added.3.refs_0_), channel_id=1, source_target_pairs={{0,128},{8,136},{16,144},{24,152},{32,160},{40,168},{48,176},{56,1... | collective-permute-start | bytes 159752 | tf_op jit(solution)/shard_map/ppermute | solution.py:234
  14.1 9.5 %collective-permute-start.4 = (f32[104,128]{1,0:T(8,128)S(1)}, f32[104,128]{1,0:T(8,128)S(1)}, u32[]{:S(2)}, u32[]{:S(2)}) collective-permute-start(f32[104,128]{1,0:T(8,128)S(1)} %added.4.refs_0_), channel_id=1, source_target_pairs={{0,64},{8,72},{16,80},{24,88},{32,96},{40,104},{48,112},{56,120},{... | collective-permute-start | bytes 159752 | tf_op jit(solution)/shard_map/ppermute | solution.py:234
  23.6 5.1 %collective-permute-start.5 = (f32[104,128]{1,0:T(8,128)S(1)}, f32[104,128]{1,0:T(8,128)S(1)}, u32[]{:S(2)}, u32[]{:S(2)}) collective-permute-start(f32[104,128]{1,0:T(8,128)S(1)} %added.5.held), channel_id=1, source_target_pairs={{0,32},{8,40},{16,48},{24,56},{32,0},{40,8},{48,16},{56,24},{64,96... | collective-permute-start | bytes 159752 | tf_op jit(solution)/shard_map/ppermute | solution.py:234
